TPU v7x, 256 devices: a whole 4x4x8 slice. The times are simulated.
256 devices in a mesh: shuf: 4 (over y_lo, core), key: 64 (over x, z, y_hi).
Axes of the slice: x: 4, y: 4 (y_hi: 2, y_lo: 2; y = y_hi * 2 + y_lo), z: 8, core: 2. Of those that a mesh axis runs over, the one named last changes fastest.
Arguments:
- embeddings: bfloat16 [32768, 1024], P(('shuf', 'key')), may hold values from -200 to 200
- labels: int32 [32768], P(('shuf', 'key')), may hold values from 0 to 2047
- order: int32 [256, 128], P(('shuf', 'key')), may hold values from 0 to 127, each once within a row
- head_weight: bfloat16 [1024, 512], replicated, may hold values from -0.1875 to 0.1875
Outputs:
- grad_embeddings: bfloat16 [32768, 1024], P(('shuf', 'key'))
- grad_head: float32 [1024, 512], P('key')
All inputs are finite; a program needn't handle non-finite values.
Results may differ from a plain program's by a relative error of at most 0.0075.
Values may be sent and summed in bfloat16 or wider, within the bound.
No kernel may reach another device: no remote copies, remote signals or barrier semaphores. Data moves between devices by JAX's collectives and lax.ppermute only.
A program may use at most 64 MiB of HBM per device.

v0:
```python
import jax
import jax.numpy as jnp
from jax import lax
from jax.sharding import PartitionSpec as P

exponent_divisor = 0.1
loss_scale = 64.0
epsilon = 1e-06


def tile_terms(query_embeddings, anchor_labels, anchor_index, piece_keys, piece_labels):
    piece_rows = piece_keys.shape[0]
    cosine_score_table = (
        lax.dot_general(
            query_embeddings,
            piece_keys,
            (((1,), (1,)), ((), ())),
            preferred_element_type=jnp.float32,
        )
        / exponent_divisor
    )
    column = jnp.arange(piece_rows, dtype=jnp.int32)
    itself = anchor_index[:, None] == column[None, :]
    exponent = jnp.where(itself, 0.0, jnp.exp(cosine_score_table))
    positive = jnp.logical_and(
        anchor_labels[:, None] == piece_labels[None, :], jnp.logical_not(itself)
    ).astype(jnp.float32)
    return (exponent, positive)


def body(embeddings, labels, order, head_weight):
    row_count = embeddings.shape[0]
    routing = order[0]
    sent_rows = jnp.take(embeddings, routing, axis=0)
    sent_labels = jnp.take(labels, routing, axis=0)
    group_rows, group_labels = (
        lax.all_to_all(sent_rows, "shuf", split_axis=0, concat_axis=0, tiled=True),
        lax.all_to_all(sent_labels, "shuf", split_axis=0, concat_axis=0, tiled=True),
    )
    projected = jnp.dot(group_rows, head_weight, preferred_element_type=jnp.float32)
    row_norm = jnp.sqrt(jnp.sum(projected * projected, axis=1, keepdims=True) + epsilon)
    direction = projected / row_norm
    normed = direction.astype(jnp.bfloat16)
    anchor_index = lax.axis_index("key") * row_count + jnp.arange(row_count, dtype=jnp.int32)
    pieces = (
        lax.all_gather(normed, "key", axis=0, tiled=True),
        lax.all_gather(group_labels, "key", axis=0, tiled=True),
    )
    exponent, positive = tile_terms(normed, group_labels, anchor_index, pieces[0], pieces[1])
    totals = jnp.sum(exponent, axis=1)
    counts = jnp.sum(positive, axis=1)
    floor_count = jnp.maximum(counts, 1.0)
    soft_weight = loss_scale * counts / (floor_count * totals)
    pos_weight = loss_scale / floor_count
    all_soft, all_pos = (
        lax.all_gather(soft_weight, "key", axis=0, tiled=True),
        lax.all_gather(pos_weight, "key", axis=0, tiled=True),
    )
    pieces = (
        lax.all_gather(normed, "key", axis=0, tiled=True),
        lax.all_gather(group_labels, "key", axis=0, tiled=True),
    )
    exponent, positive = tile_terms(normed, group_labels, anchor_index, pieces[0], pieces[1])
    coefficient = (
        (soft_weight[:, None] + all_soft[None, :]) * exponent
        - (pos_weight[:, None] + all_pos[None, :]) * positive
    ).astype(jnp.bfloat16)
    positive_partner = jnp.dot(coefficient, pieces[0], preferred_element_type=jnp.float32)
    positive_pull_derivative = positive_partner / exponent_divisor
    along = jnp.sum(direction * positive_pull_derivative, axis=1, keepdims=True)
    slopes = ((positive_pull_derivative - direction * along) / row_norm).astype(jnp.bfloat16)
    grad_rows = lax.dot_general(
        slopes, head_weight, (((1,), (1,)), ((), ())), preferred_element_type=jnp.float32
    ).astype(jnp.bfloat16)
    returned = lax.all_to_all(grad_rows, "shuf", split_axis=0, concat_axis=0, tiled=True)
    grad_embeddings = jnp.zeros_like(embeddings).at[routing].set(returned)
    summed_all = lax.psum(
        lax.dot_general(
            group_rows, slopes, (((0,), (0,)), ((), ())), preferred_element_type=jnp.float32
        ).astype(jnp.bfloat16),
        "shuf",
    ).astype(jnp.float32)
    grad_head = lax.psum_scatter(summed_all, "key", scatter_dimension=0, tiled=True)
    return (grad_embeddings, grad_head / loss_scale)


def solution(mesh):
    return jax.shard_map(
        body,
        mesh=mesh,
        in_specs=(P(("shuf", "key"), None), P(("shuf", "key")), P(("shuf", "key"), None), P()),
        out_specs=(P(("shuf", "key"), None), P("key", None)),
        check_vma=False,
    )
```

profile of v0, /device:TPU:8, one launch (start us, length us, event | category | flops | bytes accessed | tf_op | source)
XLA Modules:
  0.0 990.7 jit_solution(10155050195612298073)
XLA Ops:
  7.2 0.0 copy-start
  7.2 0.0 copy-start.2
  7.2 0.0 copy-start.1
  7.2 0.0 all-gather.5.cloned.1.call-start
  7.2 0.7 fusion.16
  8.0 0.7 squeeze.9
  8.7 2.0 gather_fusion.1
  10.8 0.1 broadcast_select_fusion
  10.9 8.9 all_to_all.27
  19.8 0.0 copy-done
  19.8 0.4 multiply_reduce_fusion.1
  20.2 0.8 fusion.18
  21.0 0.0 all-gather.5.cloned.1.call-update
  21.0 0.5 broadcast.125
  21.5 0.0 copy-done.2
  21.5 0.6 reduce.10
  22.1 0.1 squeeze.8
  22.2 0.0 copy-done.1
  22.2 1.2 gather_fusion
  23.4 0.1 gather.13
  23.5 0.6 and_select_fusion
  24.1 4.9 all-to-all-start
  28.9 0.0 all-reduce.2.cloned.1.call-start
  28.9 1.7 all-to-all-done
  30.6 0.1 reshape.148
  30.7 0.6 reduce.11
  31.3 0.1 eq.14
  31.4 181.5 %all-gather = s32[64,1,128]{2,1,0:T(1,128)S(1)} all-gather(s32[1,1,128]{2,1,0:T(1,128)S(1)} %reshape.148), channel_id=1, replica_groups=mesh['shuf'=4,'key'=64] {'key'}, dimensions={0}, use_global_device_ids=true | all-gather | bytes 33280 | tf_op jit(solution)/shard_map/all_gather | solution.py:47
  212.8 1.4 convert_reduce_fusion
  214.2 0.0 all-gather.5.cloned.1.call-done
  214.2 0.0 copy-start.3
  214.2 6.6 fusion.19
  220.9 173.1 %all-gather.2 = f32[64,1,128]{2,1,0:T(1,128)S(1)} all-gather(f32[1,1,128]{2,1,0:T(1,128)S(1)} %bitcast.36), channel_id=1, replica_groups=mesh['shuf'=4,'key'=64] {'key'}, dimensions={0}, use_global_device_ids=true | all-gather | bytes 33280 | tf_op jit(solution)/shard_map/all_gather | solution.py:57
  394.0 176.6 %all-gather.1 = f32[64,1,128]{2,1,0:T(1,128)S(1)} all-gather(f32[1,1,128]{2,1,0:T(1,128)S(1)} %bitcast.35), channel_id=1, replica_groups=mesh['shuf'=4,'key'=64] {'key'}, dimensions={0}, use_global_device_ids=true | all-gather | bytes 33280 | tf_op jit(solution)/shard_map/all_gather | solution.py:56
  570.6 0.0 copy-done.3
  570.6 2.3 multiply_reduce_fusion
  572.9 1.5 convolution_convert_fusion
  574.4 0.0 all-reduce.2.cloned.1.call-update
  574.5 0.0 reduce-scatter.2.cloned.1.call-start
  574.5 39.0 %all-reduce.2.cloned.1.call-done = bf16[1024,512]{1,0:T(8,128)(2,1)} async-done(((bf16[1024,512]{1,0:T(8,128)(2,1)}), bf16[1024,512]{1,0:T(8,128)(2,1)}) %all-reduce.2.cloned.1.call-update) | async-done | bytes 1048592 | tf_op jit(solution)/shard_map/psum | solution.py:77
  613.5 2.9 convert_element_type.28
  616.4 0.0 reduce-scatter.2.cloned.1.call-update
  616.4 0.5 convolution_convert_fusion.1
  616.9 7.9 all_to_all.28
  624.8 1.8 scatter_custom_fusion
  626.6 356.3 %reduce-scatter.2.cloned.1.call-done = f32[16,512]{1,0:T(8,128)} async-done(((f32[1024,512]{1,0:T(8,128)}), f32[16,512]{1,0:T(8,128)}) %reduce-scatter.2.cloned.1.call-update) | async-done | bytes 32784 | tf_op jit(solution)/shard_map/reduce_scatter | solution.py:83
  982.8 1.4 broadcast_multiply_fusion
  (5 shorter events, 0.0 us)
Async XLA Ops:
  7.2 12.7 %copy-start = (bf16[1024,512]{1,0:T(8,128)(2,1)S(1)}, bf16[1024,512]{1,0:T(8,128)(2,1)}, u32[]{:S(2)}) copy-start(bf16[1024,512]{1,0:T(8,128)(2,1)} %param.7) | copy-start | bytes 3145732
  7.2 14.3 %copy-start.2 = (s32[1,128]{1,0:T(1,128)S(1)}, s32[1,128]{1,0:T(1,128)}, u32[]{:S(2)}) copy-start(s32[1,128]{1,0:T(1,128)} %param.6) | copy-start | bytes 1540
  7.2 15.0 %copy-start.1 = (s32[128]{0:T(128)S(1)}, s32[128]{0:T(128)}, u32[]{:S(2)}) copy-start(s32[128]{0:T(128)} %param.5) | copy-start | bytes 1540
  7.2 207.0 %all-gather.5.cloned.1.call-start = ((), (), s32[]{:S(2)}) async-start(), calls=%async_computation.4 | async-start | bytes 8519680 | tf_op jit(solution)/shard_map/all_gather | solution.py:46
  24.1 6.5 all-to-all-start
  28.9 584.6 %all-reduce.2.cloned.1.call-start = ((), (), s32[]{:S(2)}) async-start(), calls=%async_computation.5 | async-start | bytes 2097152 | tf_op jit(solution)/shard_map/psum | solution.py:77
  214.2 356.4 %copy-start.3 = (bf16[8192,512]{1,0:T(8,128)(2,1)S(1)}, bf16[8192,512]{1,0:T(8,128)(2,1)}, u32[]{:S(2)}) copy-start(bf16[8192,512]{1,0:T(8,128)(2,1)} %all-gather.5.cloned.1.call-done) | copy-start | bytes 25165828
  574.5 408.4 %reduce-scatter.2.cloned.1.call-start = ((), (), s32[]{:S(2)}) async-start(), calls=%async_computation.6 | async-start | bytes 2129920 | tf_op jit(solution)/shard_map/reduce_scatter | solution.py:83
Sparse Core Ops, SparseCore 0:
  21.1 148.5 all-gather.4
  574.6 38.8 all-reduce.1
  616.5 366.2 reduce-scatter.1
where the time goes:
time: 991 us
  blocking collectives  548 us (55%)
  waiting for transfers between devices  397 us (40%)
  between operations  13.8 us (1%)
  matrix products  11.3 us (1%)
    reduce_scatter x1, waiting for transfers between devices, body(): lax.psum_scatter(summed_all, 'key', scatter_dimension=0, tiled=True)  356 us
    all_gather x1, blocking collectives, body(): lax.all_gather(group_labels, 'key', axis=0, tiled=True)  181 us
    all_gather x1, blocking collectives, body(): lax.all_gather(soft_weight, 'key', axis=0, tiled=True)  177 us
    all_gather x1, blocking collectives, body(): lax.all_gather(pos_weight, 'key', axis=0, tiled=True)  173 us
    psum x1, waiting for transfers between devices, body(): lax.psum(lax.dot_general(group_rows, slopes, (((0,), (0,)), ((), ())), pr...  39 us
  transfers between devices with their start and end apart: 4, of which 3 were waited for; matrix products, arithmetic and copies ran while one was open for 1% of the time, Pallas kernels for 0%

commit v1 on v0

--- a/solution.py
+++ b/solution.py
@@ -52,9 +52,18 @@
     floor_count = jnp.maximum(counts, 1.0)
     soft_weight = loss_scale * counts / (floor_count * totals)
     pos_weight = loss_scale / floor_count
+    shape_works = lambda device_axis, frame_in, dim_at: jnp.concatenate(
+        lax.all_to_all(
+            jnp.stack([frame_in for _ in range(lax.axis_size(device_axis))]),
+            axis_name=device_axis,
+            split_axis=0,
+            concat_axis=0,
+        ),
+        axis=dim_at,
+    )
     all_soft, all_pos = (
         lax.all_gather(soft_weight, "key", axis=0, tiled=True),
-        lax.all_gather(pos_weight, "key", axis=0, tiled=True),
+        shape_works("key", pos_weight, 0),
     )
     pieces = (
         lax.all_gather(normed, "key", axis=0, tiled=True),

time: 991 us -> 834 us (0.84)
  blocking collectives: 548 us -> 379 us
    all_gather x1 -> x0, blocking collectives: 173 us -> none  [body(): lax.all_gather(pos_weight, 'key', axis=0, tiled=True)]
  transfers between devices with their start and end apart: 4 -> 5, of which waited for: 3 -> 3; matrix products, arithmetic and copies ran while one was open for 1% -> 1% of each run, Pallas kernels for 0% -> 0%
where the time goes in v1:
time: 834 us
  waiting for transfers between devices  397 us (48%)
  blocking collectives  379 us (45%)
  matrix products  17.6 us (2%)
  between operations  13.8 us (2%)
  starting transfers between devices  9.57 us (1%)
  other arithmetic  8.99 us (1%)
    reduce_scatter x1, waiting for transfers between devices, body(): lax.psum_scatter(summed_all, 'key', scatter_dimension=0, tiled=True)  356 us
    all_gather x1, blocking collectives, body(): lax.all_gather(group_labels, 'key', axis=0, tiled=True)  181 us
    all_gather x1, blocking collectives, body(): lax.all_gather(soft_weight, 'key', axis=0, tiled=True)  181 us
    psum x1, waiting for transfers between devices, body(): lax.psum(lax.dot_general(group_rows, slopes, (((0,), (0,)), ((), ())), pr...  39.2 us
  transfers between devices with their start and end apart: 5, of which 3 were waited for; matrix products, arithmetic and copies ran while one was open for 1% of the time, Pallas kernels for 0%

profile of v1, /device:TPU:8, one launch (start us, length us, event | category | flops | bytes accessed | tf_op | source)
XLA Modules:
  0.0 833.5 jit_solution(3737672986153818868)
XLA Ops:
  7.2 0.0 copy-start
  7.2 0.0 copy-start.2
  7.2 0.0 copy-start.1
  7.2 0.0 all-gather.4.cloned.1.call-start
  7.2 0.7 fusion.16
  8.0 0.7 squeeze.9
  8.7 2.0 gather_fusion.1
  10.8 0.1 broadcast_select_fusion
  10.9 8.9 %all_to_all.33 = bf16[4,32,1024]{2,1,0:T(8,128)(2,1)S(1)} all-to-all(bf16[4,32,1024]{2,1,0:T(8,128)(2,1)S(1)} %broadcast_select_fusion), channel_id=1, replica_groups=mesh['shuf'=4,'key'=64] {'shuf'}, dimensions={0} | all-to-all | bytes 524288 | tf_op jit(solution)/shard_map/all_to_all | solution.py:37
  19.8 0.0 copy-done
  19.8 0.4 multiply_reduce_fusion.1
  20.2 0.8 fusion.18
  21.0 0.0 all-gather.4.cloned.1.call-update
  21.0 0.5 broadcast.132
  21.5 0.0 copy-done.2
  21.5 0.6 reduce.10
  22.1 0.1 squeeze.8
  22.2 0.0 copy-done.1
  22.2 1.2 gather_fusion
  23.4 0.1 gather.13
  23.5 0.6 and_select_fusion
  24.1 4.9 all-to-all-start
  28.9 1.7 all-to-all-done
  30.6 0.1 reshape.155
  30.7 0.6 reduce.11
  31.3 0.1 eq.14
  31.4 181.5 %all-gather = s32[64,1,128]{2,1,0:T(1,128)S(1)} all-gather(s32[1,1,128]{2,1,0:T(1,128)S(1)} %reshape.155), channel_id=1, replica_groups=mesh['shuf'=4,'key'=64] {'key'}, dimensions={0}, use_global_device_ids=true | all-gather | bytes 33280 | tf_op jit(solution)/shard_map/all_gather | solution.py:47
  212.8 1.4 convert_reduce_fusion
  214.2 0.0 all-gather.4.cloned.1.call-done
  214.2 8.4 %fusion.19 = (f32[128]{0:T(128)S(1)}, f32[128,8192]{1,0:T(8,128)}) fusion(bf16[128,512]{1,0:T(8,128)(2,1)} %fusion.18, bf16[8192,512]{1,0:T(8,128)(2,1)} %all-gather.4.cloned.1.call-done, s32[128]{0:T(128)S(1)} %iota_add_fusion), kind=kOutput, calls=%fused_computation.44 | convolution fusion | flops 1077936000 | bytes 12715008 | tf_op jit(solution)/shard_map/dot_general | solution.py:14
  222.7 0.6 stack.2
  223.3 4.6 all-to-all-start.2
  227.9 0.0 all-reduce.2.cloned.1.call-start
  227.9 180.7 %all-gather.1 = f32[64,1,128]{2,1,0:T(1,128)S(1)} all-gather(f32[1,1,128]{2,1,0:T(1,128)S(1)} %bitcast.34), channel_id=1, replica_groups=mesh['shuf'=4,'key'=64] {'key'}, dimensions={0}, use_global_device_ids=true | all-gather | bytes 33280 | tf_op jit(solution)/shard_map/all_gather | solution.py:65
  408.7 0.0 all-to-all-done.2
  408.7 6.8 multiply_reduce_fusion
  415.5 1.5 convolution_convert_fusion
  417.0 0.0 all-reduce.2.cloned.1.call-update
  417.0 0.0 reduce-scatter.2.cloned.1.call-start
  417.1 39.2 %all-reduce.2.cloned.1.call-done = bf16[1024,512]{1,0:T(8,128)(2,1)} async-done(((bf16[1024,512]{1,0:T(8,128)(2,1)}), bf16[1024,512]{1,0:T(8,128)(2,1)}) %all-reduce.2.cloned.1.call-update) | async-done | bytes 1048592 | tf_op jit(solution)/shard_map/psum | solution.py:86
  456.2 2.9 convert_element_type.28
  459.1 0.0 reduce-scatter.2.cloned.1.call-update
  459.1 0.5 convolution_convert_fusion.1
  459.6 7.9 all_to_all.34
  467.5 1.8 scatter_custom_fusion
  469.3 356.3 %reduce-scatter.2.cloned.1.call-done = f32[16,512]{1,0:T(8,128)} async-done(((f32[1024,512]{1,0:T(8,128)}), f32[16,512]{1,0:T(8,128)}) %reduce-scatter.2.cloned.1.call-update) | async-done | bytes 32784 | tf_op jit(solution)/shard_map/reduce_scatter | solution.py:92
  825.6 1.4 broadcast_multiply_fusion
  (5 shorter events, 0.0 us)
Async XLA Ops:
  7.2 12.7 %copy-start = (bf16[1024,512]{1,0:T(8,128)(2,1)S(1)}, bf16[1024,512]{1,0:T(8,128)(2,1)}, u32[]{:S(2)}) copy-start(bf16[1024,512]{1,0:T(8,128)(2,1)} %param.7) | copy-start | bytes 3145732
  7.2 14.3 %copy-start.2 = (s32[1,128]{1,0:T(1,128)S(1)}, s32[1,128]{1,0:T(1,128)}, u32[]{:S(2)}) copy-start(s32[1,128]{1,0:T(1,128)} %param.6) | copy-start | bytes 1540
  7.2 15.0 %copy-start.1 = (s32[128]{0:T(128)S(1)}, s32[128]{0:T(128)}, u32[]{:S(2)}) copy-start(s32[128]{0:T(128)} %param.5) | copy-start | bytes 1540
  7.2 207.0 %all-gather.4.cloned.1.call-start = ((), (), s32[]{:S(2)}) async-start(), calls=%async_computation.5 | async-start | bytes 8519680 | tf_op jit(solution)/shard_map/all_gather | solution.py:46
  24.1 6.5 all-to-all-start
  223.3 185.4 %all-to-all-start.2 = ((f32[64,1,128]{2,1,0:T(1,128)}), f32[64,1,128]{2,1,0:T(1,128)S(1)}, u32[]{:S(2)}, u32[]{:S(2)}) async-start(f32[64,1,128]{2,1,0:T(1,128)} %stack.2), calls=%async_computation.2 | async-start | bytes 65536 | tf_op jit(solution)/shard_map/all_to_all | solution.py:56
  227.9 228.3 %all-reduce.2.cloned.1.call-start = ((), (), s32[]{:S(2)}) async-start(), calls=%async_computation.6 | async-start | bytes 2097152 | tf_op jit(solution)/shard_map/psum | solution.py:86
  417.0 408.6 %reduce-scatter.2.cloned.1.call-start = ((), (), s32[]{:S(2)}) async-start(), calls=%async_computation.7 | async-start | bytes 2129920 | tf_op jit(solution)/shard_map/reduce_scatter | solution.py:92
Sparse Core Ops, SparseCore 0:
  21.1 148.5 all-gather.3
  417.1 39.0 all-reduce.1
  459.3 366.2 reduce-scatter.1
